TPU v7x, 128 devices: a whole 4x4x4 slice. The times are simulated.
128 devices in a mesh: sub: 32 (over y, z, core), rep: 4 (over x).
Axes of the slice: x: 4, y: 4, z: 4, core: 2. Of those that a mesh axis runs over, the one named last changes fastest.
Arguments:
- regions: bfloat16 [512, 512, 256], P('rep', 'sub'), may hold values from -6 to 6
- leaf_map: int32 [512], P('sub'), may hold values from 0 to 15, as said below
- leaf_bond_weight: bfloat16 [128, 4, 256, 1024], P(('sub', 'rep')), may hold values from -0.375 to 0.375
- mid_weight: bfloat16 [32, 4, 1024, 1024], P('sub', 'rep'), may hold values from -0.1875 to 0.1875
- upper_weight: bfloat16 [32, 1024, 2, 1024], P('sub'), may hold values from -0.1875 to 0.1875
- head_cotangent: float32 [512, 1024], P('rep', 'sub'), may hold values from -0.75 to 0.75
Outputs:
- leaf_grad: bfloat16 [128, 4, 256, 1024], P(('sub', 'rep'))
- middle_weight_gradient: bfloat16 [32, 4, 1024, 1024], P('sub', 'rep')
- upper_grad: bfloat16 [32, 1024, 2, 1024], P('sub', 'rep')
Inputs may be any that keep to these rules, and one draw needn't show every extreme that they name: `leaf_map`: each aligned block of 16 entries is a permutation of 0 .. 15.
All inputs are finite; a program needn't handle non-finite values.
Results may differ from a plain program's by a relative error of at most 0.04.
Values may be sent and summed in bfloat16 or wider, within the bound.
A program may use at most 128 MiB of HBM per device.

v0:
```python
import jax
import jax.numpy as jnp
from jax import lax
from jax.experimental import pallas as pl
from jax.experimental.pallas import tpu as pltpu
from jax.sharding import PartitionSpec as P

F32 = jnp.float32
BF = jnp.bfloat16
MESH = pl.DeviceIdType.MESH
EPSILON = 1e-06
VMEM_LIMIT = 58500000
D = 1024
F = 256
B = 128
REPS = 4
SUBS = 32
LEVELS = 5
ALL = REPS * B
WIDTH = [D // 2 ** (j + 1) for j in range(LEVELS)] + [D // SUBS]
COLUMN = [D - 2 * WIDTH[j] for j in range(LEVELS)] + [D - D // SUBS]
CHUNK = [2 * WIDTH[j] for j in range(LEVELS)] + [WIDTH[5]]
GROUP = [2 ** (j + 1) for j in range(LEVELS)] + [SUBS]


def nn(a, b):
    return jnp.dot(a, b, preferred_element_type=F32)


def nt(a, b):
    return lax.dot_general(a, b, (((1,), (1,)), ((), ())), preferred_element_type=F32)


def fold(values):
    return jnp.sum(values.reshape(values.shape[0] // 8, 8, values.shape[1]), axis=0)


def column_sum(values):
    return jnp.sum(values, axis=0, keepdims=True)


def factor_of(squares):
    return lax.rsqrt(column_sum(squares) * (1.0 / D) + EPSILON)


def at(index, size):
    return pl.ds(pl.multiple_of(index * size, size), size)


def lanes_of(i):
    return slice(i * B, (i + 1) * B)


OFFSET = (0, 1, 3, 2)
BACK = (0, 2, 1, 3)


STEP_SLOT = {(dy, dz): 4 * dy + dz for dy in range(4) for dz in range(4)}
EXTENT = ((1, 1), (1, 2), (1, 4), (2, 4), (4, 4))


def steps_of(level):
    ny, nz = EXTENT[level]
    steps = [(dy, dz) for dy in range(ny) for dz in range(nz) if dy or dz]
    return sorted(steps, key=lambda d: min(d[0], ny - d[0]) + min(d[1], nz - d[1]))


def others(f):
    p01 = f[0] * f[1]
    p23 = f[2] * f[3]
    return [f[1] * p23, f[0] * p23, p01 * f[3], p01 * f[2]]


def split_tile(row):
    high = row.astype(BF).astype(F32)
    index = lax.broadcasted_iota(jnp.int32, (16, B), 0)
    tile = jnp.where(index == 0, high, jnp.where(index == 1, row - high, 0.0))
    return tile.astype(BF)


def kernel(
    map_ref, reg_hbm, lw_hbm, mw_hbm, uw_hbm, cot_hbm,
    WT, LM, CR, XT, OU,
    R, Q, XS, XR, LW, LWT, MW, MWT, UW, WN, CF, FK, RL, MS, MR,
    A0, A1, A2, A3, A4, A5, UL, UR, JJ, GP, GB, WP, BO, BI,
    BS1, BS2, BS3, BR1, BR2, BR3,
    GX, AX, CS, LB, LO, H0, R0, PR, PM, WF, W4, UF, GH, PB,
    load_sem, local_sem, x1s, x1r, x2s, x2r, x3s, x3r, h0s, h0r, fs, fr, ff, fo, bs, br, bos, bis,
    axs, axr, aps, apr, gxs, gxr, gx0, gxt, pss, prs, cfs, cfr, w1s, w1r, w2s, w2r, w3s, w3r, w4s, w4r,
):
    A = [A0, A1, A2, A3, A4, A5]
    BS = [None, BS1, BS2, BS3]
    BR = [None, BR1, BR2, BR3]
    s = lax.axis_index("sub")
    p = lax.axis_index("rep")

    def to_rep(src, dst, send, recv, peer):
        pltpu.make_async_remote_copy(
            src_ref=src, dst_ref=dst, send_sem=send, recv_sem=recv,
            device_id={"rep": peer}, device_id_type=MESH,
        ).start()

    def to_sub(src, dst, send, recv, peer):
        pltpu.make_async_remote_copy(
            src_ref=src, dst_ref=dst, send_sem=send, recv_sem=recv,
            device_id={"sub": peer}, device_id_type=MESH,
        ).start()

    def await_bytes(ref, sem):
        pltpu.make_async_copy(ref, ref, sem).wait()

    c = lax.rem(s, 2)
    z = lax.rem(s // 2, 4)
    y = s // 8
    partner = s + 1 - 2 * c

    def upper_part(t):
        return pltpu.make_async_copy(uw_hbm.at[128 * t : 128 * (t + 1)], UW.at[t % 4], load_sem.at[4 + t % 4])

    loads = [
        pltpu.make_async_copy(src, dst, load_sem.at[i])
        for i, (src, dst) in enumerate([(reg_hbm, R), (lw_hbm, LW), (mw_hbm, MW), (cot_hbm, CF.at[y, z, c])])
    ]
    loads[0].start()
    loads[3].start()
    for t in range(4):
        upper_part(t).start()
    loads[1].start()
    loads[2].start()

    barrier = pltpu.get_barrier_semaphore()

    def greet_sub(i, carry):
        pl.semaphore_signal(
            barrier, inc=1, device_id={"sub": lax.rem(s + i, SUBS)}, device_id_type=MESH
        )
        return carry

    def greet_rep(i, carry):
        pl.semaphore_signal(
            barrier, inc=1, device_id={"rep": lax.rem(p + i, REPS)}, device_id_type=MESH
        )
        return carry

    lax.fori_loop(1, SUBS, greet_sub, 0)
    lax.fori_loop(1, REPS, greet_rep, 0)

    column = lax.broadcasted_iota(jnp.int32, (16, 256), 1)
    sample = lax.broadcasted_iota(jnp.int32, (16, 256), 0)
    for l in range(16):
        wanted = sample * 16 + map_ref[l]
        Q[16 * l : 16 * l + 16, :] = jnp.where(column == wanted, 1.0, 0.0).astype(BF)
    loads[0].wait()

    for q in range(8):
        got = nn(Q[...], R[256 * q : 256 * (q + 1), :]).astype(BF)
        for l in range(16):
            XS[l // 4, l % 4, 16 * q : 16 * q + 16, :] = got[16 * l : 16 * l + 16, :]
    pl.semaphore_wait(barrier, SUBS - 1 + REPS - 1)

    def source(i):
        return lax.rem(p + OFFSET[i], REPS)

    for i in range(1, REPS):
        peer = source(i)
        to_rep(XS.at[peer], XR.at[:, lanes_of(BACK[i]), :], x1s, x1r.at[BACK[i]], peer)
    own_slots = pltpu.make_async_copy(XS.at[p], XR.at[:, 0:B, :], local_sem.at[0])
    own_slots.start()

    for t in range(8):
        upper_part(t).wait()
        for q in range(4):
            rows = slice(128 * t + 32 * q, 128 * t + 32 * (q + 1))
            WN[:, rows, :] = jnp.swapaxes(UW[t % 4, 32 * q : 32 * (q + 1)], 0, 1)
        if t < 4:
            upper_part(t + 4).start()
    for side in range(2):
        for t in range(4):
            rows = slice(256 * t, 256 * (t + 1))
            WF[y, z, c, side, :, rows] = WN[side, rows, 896:1024].T[64:128, :]

    def chip(dy, dz):
        return (lax.rem(y + dy, 4) * 4 + lax.rem(z + dz, 4)) * 2 + c

    for k in range(1, 4):
        ref = WF.at[y, z, c, 0]
        to_sub(ref, ref, w1s, w1r.at[0], chip(k, 0))
        ref = WF.at[y, z, c, 1]
        to_sub(ref, ref, w1s, w1r.at[1], chip(0, k))
    for side in range(2):
        ref = WF.at[y, z, c, side]
        for way, step in ((0, 1), (1, 3)):
            to_sub(ref, ref, w2s, w2r.at[side, way], chip(0, step) if side == 0 else chip(step, 0))
    loads[3].wait()
    for k in range(1, 4):
        ref = CF.at[y, z, c]
        to_sub(ref, ref, cfs.at[0], cfr.at[0], chip(k, 0))

    def maps_to_neighbours():
        for side in range(2):
            await_bytes(WF.at[0:3, 0, 0, side], w1r.at[side])
            for k in range(1, 4):
                ref = WF.at[lax.rem(y + k, 4), z, c, 0] if side == 0 else WF.at[y, lax.rem(z + k, 4), c, 1]
                for way, step in ((0, 1), (1, 3)):
                    to_sub(ref, ref, w2s, w2r.at[side, way], chip(0, step) if side == 0 else chip(step, 0))
        await_bytes(CF.at[0:3, 0, 0], cfr.at[0])
        ref = CF.at[:, z, c]
        for k in range(1, 4):
            to_sub(ref, ref, cfs.at[1], cfr.at[1], chip(0, k))

    def maps_to_opposite():
        for side in range(2):
            for way, step in ((0, 1), (1, 3)):
                half = slice(2 * way, 2 * way + 2)
                if side == 0:
                    came = lax.rem(z + 4 - step, 4)
                    await_bytes(WF.at[:, came, c, 0], w2r.at[side, way])
                    ref = WF.at[half, came, c, 0]
                    to_sub(ref, ref, w3s, w3r.at[side, way], chip(0, step))
                else:
                    came = lax.rem(y + 4 - step, 4)
                    await_bytes(WF.at[came, :, c, 1], w2r.at[side, way])
                    ref = WF.at[came, half, c, 1]
                    to_sub(ref, ref, w3s, w3r.at[side, way], chip(step, 0))

    def maps_arrived():
        await_bytes(CF.at[:, 0:3, 0], cfr.at[1])
        to_sub(CF.at[:, :, c], CF.at[:, :, c], cfs.at[2], cfr.at[2], partner)
        for side in range(2):
            for way in range(2):
                await_bytes(WF.at[0:2, 0, 0, 0], w3r.at[side, way])

    def maps_to_partner(part):
        for row in part:
            to_sub(WF.at[row, :, c], WF.at[row, :, c], w4s, w4r, partner)

    GP[...] = jnp.zeros(GP.shape, BF)
    loads[1].wait()

    def turn_leaf(i, carry):
        k, t = i // 4, lax.rem(i, 4)
        LWT[k, at(t, 256), :] = LW[k, :, at(t, 256)].T
        return carry

    lax.fori_loop(0, 16, turn_leaf, 0)
    loads[2].wait()

    def turn_mid(i, carry):
        a, b = i // 4, lax.rem(i, 4)
        MWT[at(b, 256), at(a, 256)] = MW[at(a, 256), at(b, 256)].T
        return carry

    lax.fori_loop(0, 16, turn_mid, 0)

    def leaf_blocks(lanes):
        n = lanes.stop - lanes.start
        squares = jnp.zeros((8, n), F32)
        for t in range(4):
            rows = slice(256 * t, 256 * (t + 1))
            product = None
            for k in range(4):
                factor = 1.0 + nt(LWT[k, rows, :], XR[k, lanes, :])
                FK[k, rows, lanes] = factor.astype(BF)
                product = factor if product is None else product * factor
            LB[rows, 0:n] = product
            squares = squares + fold(product * product)
        r = factor_of(squares)
        RL[:, lanes] = jnp.broadcast_to(r, (8, n))
        for t in range(4):
            rows = slice(256 * t, 256 * (t + 1))
            LM[rows, lanes] = (LB[rows, 0:n] * r).astype(BF)
        for t in range(4):
            rows = slice(256 * t, 256 * (t + 1))
            value = nn(MWT[rows, :], LM[:, lanes]).astype(BF)
            for b in range(n // B):
                MS[lanes.start // B + b, rows, :] = value[:, lanes_of(b)]

    def turn_slots(lanes):
        for k in range(4):
            XT[k, :, lanes] = XR[k, lanes, :].T

    own_slots.wait()
    leaf_blocks(slice(0, B))
    own_mid = pltpu.make_async_copy(MS.at[0], MR.at[p], local_sem.at[1])
    own_mid.start()
    for t in range(8):
        rows = slice(128 * t, 128 * (t + 1))
        for side in range(2):
            WT[2 * side + t // 4, 0:960, 128 * (t % 4) : 128 * (t % 4 + 1)] = WN[side, rows, 0:960].T
    for level in (2, 3):
        size = CHUNK[level]
        col = min(COLUMN[level], 896)
        count = D // size
        for side in range(2):
            for q in range(count):
                to = (q % 2 * (count // 2) + q // 2) * size
                WP[level - 2, side, to : to + size, :] = WN[side, q * size : (q + 1) * size, col : col + 128]
    turn_slots(slice(0, B))
    for blocks in ((1, 2), (3,)):
        for i in blocks:
            await_bytes(XR.at[:, lanes_of(i), :], x1r.at[i])
        lanes = slice(blocks[0] * B, (blocks[-1] + 1) * B)
        leaf_blocks(lanes)
        for i in blocks:
            to_rep(MS.at[i], MR.at[p], x2s, x2r, source(i))
        turn_slots(lanes)
        if len(blocks) == 2:
            maps_to_neighbours()

    maps_to_opposite()
    own_mid.wait()
    await_bytes(MR.at[0:3], x2r)
    for t in range(8):
        rows = slice(128 * t, 128 * (t + 1))
        product = 1.0 + MR[0, rows, :].astype(F32)
        for k in range(1, 4):
            product = product * (1.0 + MR[k, rows, :].astype(F32))
        A0[pl.ds(pl.multiple_of(c * D + t * 128, 128), 128), :] = product.astype(BF)

    own = slice(0, B)

    def spread(level, me, block):
        ref = A[level].at[at(me, block), :]
        to_sub(ref, ref, fs.at[level], fo.at[level], partner)

        for step in reversed(steps_of(level)):
            to_sub(ref, ref, fs.at[level], fr.at[level, STEP_SLOT[step]], chip_of(level, step, 1))

    def chip_of(level, step, sign):
        ny, nz = EXTENT[level]
        yy = y // ny * ny + lax.rem(lax.rem(y, ny) + (step[0] if sign > 0 else ny - step[0]), ny)
        zz = z // nz * nz + lax.rem(lax.rem(z, nz) + (step[1] if sign > 0 else nz - step[1]), nz)
        return (yy * 4 + zz) * 2 + c

    def collect(level, me, block):
        half = GROUP[level] // 2

        for step in steps_of(level):
            ref = A[level].at[at(chip_of(level, step, -1) - s + me, block), :]
            await_bytes(ref, fr.at[level, STEP_SLOT[step]])
            to_sub(ref, ref, ff.at[level], fo.at[level], partner)
        await_bytes(A[level].at[0 : half * block], fo.at[level])

    def share_rows(level):
        for i in range(1, REPS):
            if level < LEVELS:
                rows = pl.ds(pl.multiple_of(c * D + source(i) * 256, 256), 256)
                dst = AX.at[level, c, :, lanes_of(BACK[i])]
            else:
                rows = pl.ds(pl.multiple_of(source(i) * 256 + c * 128, 128), 128)
                dst = AX.at[level, 0, at(c, 128), lanes_of(BACK[i])]
            to_rep(A[level].at[rows, :], dst, axs.at[level], axr.at[level], source(i))
        for side in range(2 if level < LEVELS else 1):
            rows = pl.ds(pl.multiple_of(side * D + p * 256, 256), 256)
            copy = pltpu.make_async_copy(
                A[level].at[rows, :], AX.at[level, side, :, own], local_sem.at[2 + 2 * level + side]
            )
            copy.start()
            kept.append(copy)

    def pass_rows(level):
        if level == 0:
            await_bytes(H0.at[:, 0 : 3 * B], h0r)
            for copy in message_copies:
                copy.wait()
            src, dst = H0.at[at(p, 256), :], AX.at[0, c]
        elif level < LEVELS:
            await_bytes(AX.at[level, 0, :, 0 : 3 * B], axr.at[level])
            src = dst = AX.at[level, c, :, B:ALL]
        else:
            await_bytes(AX.at[level, 0, 0:128, 0 : 3 * B], axr.at[level])
            src = dst = AX.at[level, 0, at(c, 128), B:ALL]
        to_sub(src, dst, aps.at[level], apr.at[level], partner)

    def passed(level):
        if level == 0:
            return AX.at[0, 0]
        if level < LEVELS:
            return AX.at[level, 0, :, 0 : 3 * B]
        return AX.at[level, 0, 0:128, 0 : 3 * B]

    kept = []

    def squares_of(ref, start, lanes=slice(0, B)):
        total = jnp.zeros((8, B), F32)
        for t in range(4):
            values = ref[start + 256 * t : start + 256 * (t + 1), lanes].astype(F32)
            total = total + fold(values * values)
        return total

    spread(0, c, D)
    message = A0.at[at(c, D), :]

    def leave_one(t, carry):
        rows = at(t, 128)
        rest = others([1.0 + MR[k, rows, :].astype(F32) for k in range(4)])
        for k in range(4):
            CS[k, rows, :] = rest[k].astype(BF)
        return carry

    lax.fori_loop(0, 8, leave_one, 0)

    for i in range(1, REPS):
        to_rep(message, H0.at[:, lanes_of(BACK[i])], h0s, h0r, source(i))
    for i in range(1, REPS):
        to_rep(CS.at[source(i)], LO.at[:, lanes_of(BACK[i])], x3s, x3r, source(i))
    message_copies = [
        pltpu.make_async_copy(CS.at[p], LO.at[:, own], local_sem.at[20]),
        pltpu.make_async_copy(message, H0.at[:, own], local_sem.at[21]),
    ]
    for copy in message_copies:
        copy.start()
    scales = []
    for level in range(LEVELS - 1):
        group, w, col = GROUP[level], WIDTH[level], COLUMN[level]
        collect(level, lax.rem(s, group), 2 * D // group)
        if level:
            share_rows(level)
        left = factor_of(squares_of(A[level], 0))
        right = factor_of(squares_of(A[level], D))
        scales.append((left, right))
        me = lax.rem(s, GROUP[level + 1])
        size = min(w, 256)
        for t in range(w // size):
            rows = slice(col + t * size, col + (t + 1) * size)
            ul = (nn(WT[0, rows, :], A[level][0:512, :]) + nn(WT[1, rows, :], A[level][512:D, :])) * left
            ur = (nn(WT[2, rows, :], A[level][D:1536, :]) + nn(WT[3, rows, :], A[level][1536 : 2 * D, :])) * right
            joined = (1.0 + ul) * (1.0 + ur)
            UL[rows, :] = ul
            UR[rows, :] = ur
            JJ[rows, :] = joined
            A[level + 1][pl.ds(pl.multiple_of(me * w + t * size, size), size), :] = joined.astype(BF)
        spread(level + 1, me, w)
        if level == 1:
            maps_arrived()
            maps_to_partner((0, 1))
        if level == 2:
            maps_to_partner((2, 3))

    def share_grads(level):
        w, col = WIDTH[level], COLUMN[level]
        for i in range(1, REPS):
            to_rep(
                GX.at[:, col : col + w, own], GX.at[:, col : col + w, lanes_of(BACK[i])],
                gxs.at[level], gxr.at[level], source(i),
            )

    def share_last_grads():
        for i in (1, 2):
            for side in (i - 1, 2 - i):
                to_rep(
                    GX.at[side, 0:512, own], GX.at[side, 0:512, lanes_of(BACK[i])],
                    gxs.at[0], gx0.at[BACK[i], side], source(i),
                )

    def relay_last_grads():
        for i in (1, 2):
            side = i - 1
            ref = GX.at[side, 0:512, lanes_of(BACK[i])]
            await_bytes(ref, gx0.at[BACK[i], side])
            to_rep(ref, GX.at[side, 0:512, lanes_of(3)], gxt, gx0.at[3, side], source(i))

    def scatter(level, me):
        at_chip = me // 2
        for step in reversed(steps_of(level)):
            peer = chip_of(level, step, 1)
            d = at_chip + (peer - s) // 2
            to_sub(BS[level].at[d], BR[level].at[at_chip], bs.at[level], br.at[level], peer)
        copy = pltpu.make_async_copy(
            BS[level].at[at_chip], BR[level].at[at_chip], local_sem.at[14 + level]
        )
        copy.start()
        return copy

    await_bytes(WF.at[:, :, 0], w4r)
    mine = s // 16
    block = lax.rem(s, 16)
    for g in range(4):
        cols = slice(256 * g, 256 * (g + 1))
        lanes = pl.ds(pl.multiple_of(block // 2 * 128, 128), 128)
        W4[:, cols] = WF[g, :, :, mine, 0:32, lanes].reshape(256, 128).T
    collect(4, s, 2 * D // SUBS)
    share_rows(4)
    left = factor_of(squares_of(A4, 0))
    right = factor_of(squares_of(A4, D))
    scales.append((left, right))
    squares = jnp.zeros((8, B), F32)
    for g in range(4):
        rows = slice(256 * g, 256 * (g + 1))
        ul = nn(WF[g, :, :, 0, 0:32, :].reshape(256, D), A4[0:D, :]) * left
        ur = nn(WF[g, :, :, 1, 0:32, :].reshape(256, D), A4[D : 2 * D, :]) * right
        joined = ((1.0 + ul) * (1.0 + ur)).astype(BF)
        UF[0, rows, :] = ul
        UF[1, rows, :] = ur
        A5[rows, :] = joined
        squares = squares + fold(joined.astype(F32) * joined.astype(F32))
    root_scale = factor_of(squares)
    share_rows(5)
    await_bytes(CF.at[:, :, 0], cfr.at[2])
    for g in range(4):
        rows = slice(256 * g, 256 * (g + 1))
        za = nn(WF[g, :, :, 0, 32:64, :].reshape(256, D), A5[...]) * root_scale
        zb = nn(WF[g, :, :, 1, 32:64, :].reshape(256, D), A5[...]) * root_scale
        sigma = 1.0 / (1.0 + jnp.exp(-zb))
        cotangent = CF[g].reshape(256, B)
        GH[0, rows, :] = (cotangent * sigma).astype(BF)
        GH[1, rows, :] = (cotangent * za * sigma * (1.0 - sigma)).astype(BF)
    block_rows = pl.ds(pl.multiple_of(s * 32, 32), 32)
    for side in range(2):
        GX[side, 992:1024, own] = (GH[side, block_rows, :].astype(F32) * root_scale).astype(BF)
    share_grads(5)
    turned = [GH[side].T for side in range(2)]
    total = jnp.zeros((8, B), F32)
    for t in range(4):
        rows = slice(256 * t, 256 * (t + 1))
        part = None
        for side in range(2):
            term = nn(turned[side], WF[:, :, :, side, 32:64, rows].reshape(D, 256))
            part = term if part is None else part + term
        part = part.T
        PB[rows, :] = part
        total = total + fold(part * A5[rows, :].astype(F32))
    mean = column_sum(total) * (1.0 / D)
    shift = root_scale * root_scale * mean
    dl = jnp.zeros((8, B), F32)
    dr = jnp.zeros((8, B), F32)
    for t in range(8):
        rows = slice(128 * t, 128 * (t + 1))
        ul, ur = UF[0, rows, :], UF[1, rows, :]
        v = root_scale * (PB[rows, :] - (1.0 + ul) * (1.0 + ur) * shift)
        gl = (v * (1.0 + ur)).astype(BF)
        gr = (v * (1.0 + ul)).astype(BF)
        GH[0, rows, :] = gl
        GH[1, rows, :] = gr
        dl = dl + fold(gl.astype(F32) * ul)
        dr = dr + fold(gr.astype(F32) * ur)
    root_mean = jnp.where(mine == 1, column_sum(dr), column_sum(dl)) * (1.0 / D)
    part_rows = pl.ds(pl.multiple_of(lax.rem(block, 2) * 64, 64), 64)
    PB[0:64, :] = nn(W4[part_rows, :], GH[mine])
    for side in range(2):
        GX[side, 960:992, own] = (GH[side, block_rows, :].astype(F32) * scales[4][side]).astype(BF)
    share_grads(4)

    def gathered(level, rows):
        if level == LEVELS - 1:
            return PB[rows, :]
        group = BR[level].shape[0]
        total = BR[level][0, rows, :].astype(F32)
        for g in range(1, group):
            total = total + BR[level][g, rows, :].astype(F32)
        return total

    def await_chunks(level, copy):
        if level == LEVELS - 1:
            return root_mean
        copy.wait()
        await_bytes(BR[level].at[0 : BR[level].shape[0] - 1], br.at[level])
        size = CHUNK[level]
        return column_sum(gathered(level, slice(size, size + 16))) * (1.0 / D)

    own_chunk = None
    for level in reversed(range(LEVELS - 1)):
        group, w, col = GROUP[level], WIDTH[level], COLUMN[level]
        mean = await_chunks(level + 1, own_chunk)
        side_of = lax.rem(s // GROUP[level], 2)
        r = jnp.where(side_of == 1, scales[level + 1][1], scales[level + 1][0])
        left, right = scales[level]
        size = min(w, 64)

        def node_back(t, carry):
            dl, dr = carry
            rows = pl.ds(pl.multiple_of(col + t * size, size), size)
            total = gathered(level + 1, pl.ds(pl.multiple_of(t * size, size), size))
            ul, ur = UL[rows, :], UR[rows, :]
            v = r * (total - JJ[rows, :] * (r * mean))
            gl = v * (1.0 + ur)
            gr = v * (1.0 + ul)
            GX[0, rows, own] = (gl * left).astype(BF)
            GX[1, rows, own] = (gr * right).astype(BF)
            if level == 0:
                return carry
            gl = gl.astype(BF)
            gr = gr.astype(BF)
            if level < 3:
                near = pl.ds(pl.multiple_of(col - 512 + t * size, size), size)
                GB[0, near, :] = gl
                GB[1, near, :] = gr
            else:
                GP[level - 3, 0, col - 896 : col - 896 + w, :] = gl
                GP[level - 3, 1, col - 896 : col - 896 + w, :] = gr
            return dl + fold(gl.astype(F32) * ul), dr + fold(gr.astype(F32) * ur)

        zero = jnp.zeros((8, B), F32)
        dl, dr = lax.fori_loop(0, w // size, node_back, (zero, zero))
        if level == 0:
            share_last_grads()
            break
        chunk = CHUNK[level]
        dots = [column_sum(dl), column_sum(dr)]

        def half_sums(side, parity):
            rows = pl.ds(pl.multiple_of(parity * 512, 512), 512)
            if level == 1:
                return nn(WN[side, rows, col : col + w], GB[side, col - 512 : col - 512 + w, :])
            if level == 2:
                return nn(WP[0, side, rows, :], GB[side, col - 512 : col - 512 + w, :])
            return nn(WP[level - 2, side, rows, :], GP[level - 3, side])

        for side in range(2):
            BO[level - 1, side, 0:512, :] = half_sums(side, 1 - c).astype(BF)
            BO[level - 1, side, 512:528, :] = split_tile(dots[side])
        to_sub(BO.at[level - 1], BI.at[level - 1], bos.at[level], bis.at[level], partner)
        for side in range(2):
            LB[side * 512 : (side + 1) * 512, 0:B] = half_sums(side, c)
        await_bytes(BI.at[level - 1], bis.at[level])
        quarter = group // 4
        for side in range(2):
            tile = split_tile(dots[side] + column_sum(BI[level - 1, side, 512:528, :].astype(F32)))
            chunks = slice(side * quarter, (side + 1) * quarter)
            value = (LB[side * 512 : (side + 1) * 512, 0:B] + BI[level - 1, side, 0:512, :].astype(F32)).astype(BF)
            BS[level][chunks, 0:chunk, :] = value.reshape(quarter, chunk, B)
            BS[level][chunks, chunk : chunk + 16, :] = jnp.broadcast_to(tile[None], (quarter, 16, B))
        own_chunk = scatter(level, lax.rem(s, group))
        if level > 1:
            share_grads(level)
        for done in {3: (0, 1, 2), 2: (3, 4), 1: (5,)}[level]:
            pass_rows(done)

    await_bytes(MS.at[0:3], x2s)

    def partial_sums(blocks):
        for i in blocks:
            for side in {0: (), 1: (0,), 2: (1,), 3: (0, 1)}[i]:
                await_bytes(GX.at[side, 0:512, lanes_of(i)], gx0.at[i, side])
        lanes = slice(blocks[0] * B, (blocks[-1] + 1) * B)
        for t in range(4):
            rows = slice(256 * t, 256 * (t + 1))
            value = nn(WN[1 - c, rows, 0:512], GX[1 - c, 0:512, lanes]).astype(BF)
            for b, i in enumerate(blocks):
                MS[i, rows, :] = value[:, lanes_of(b)]
        for i in blocks:
            to_sub(MS.at[i], PR.at[i], pss, prs.at[i], partner)
        for t in range(4):
            rows = slice(256 * t, 256 * (t + 1))
            PM[rows, 0 : B * len(blocks)] = nn(WN[c, rows, 0:512], GX[c, 0:512, lanes])

    partial_sums((0,))

    await_bytes(LO.at[:, 0 : 3 * B], x3r)
    for i in range(REPS):
        R0[:, lanes_of(i)] = jnp.broadcast_to(factor_of(squares_of(H0, 0, lanes_of(i))), (8, B))

    def leaf_back(blocks):
        lanes = slice(blocks[0] * B, (blocks[-1] + 1) * B)
        n = B * len(blocks)
        for i in blocks:
            await_bytes(PR.at[i], prs.at[i])
        for b, i in enumerate(blocks):
            part = lanes_of(b)
            total = jnp.zeros((8, B), F32)
            for t in range(8):
                rows = slice(128 * t, 128 * (t + 1))
                value = PM[rows, part] + PR[i, rows, :].astype(F32)
                PM[rows, part] = value
                total = total + fold(value * H0[rows, lanes_of(i)].astype(F32))
            scale0 = R0[0:1, lanes_of(i)]
            shift = scale0 * scale0 * (column_sum(total) * (1.0 / D))
            for t in range(8):
                rows = slice(128 * t, 128 * (t + 1))
                v = PM[rows, part] - H0[rows, lanes_of(i)].astype(F32) * shift
                CR[rows, lanes_of(i)] = (v * LO[rows, lanes_of(i)].astype(F32)).astype(BF)
        total = jnp.zeros((8, n), F32)
        for t in range(4):
            rows = slice(256 * t, 256 * (t + 1))
            value = nn(MW[rows, :], CR[:, lanes])
            LB[rows, 0:n] = value
            total = total + fold(value * LM[rows, lanes].astype(F32))
        mean = column_sum(total) * (1.0 / D)
        r = RL[0:1, lanes]
        for t in range(16):
            rows = slice(64 * t, 64 * (t + 1))
            v = r * (LB[rows, 0:n] - LM[rows, lanes].astype(F32) * mean)
            rest = others([FK[k, rows, lanes].astype(F32) for k in range(4)])
            for k in range(4):
                WT[k, rows, lanes] = (v * rest[k]).astype(BF)

    def await_grads(level):
        w, col = WIDTH[level], COLUMN[level]
        await_bytes(GX.at[:, col : col + w, 0 : 3 * B], gxr.at[level])

    leaf_back((0,))
    relay_last_grads()
    share_grads(1)
    partial_sums((1, 2))

    for copy in kept:
        copy.wait()
    for level in range(LEVELS + 1):
        await_bytes(passed(level), apr.at[level])
    for level in (5, 4, 3):
        await_grads(level)
    lane = lax.broadcasted_iota(jnp.int32, (256, 128), 1)
    for side in range(2):
        grads = GX[side, 896:1024, :]
        g3 = nt(AX[3, side], grads)
        g4 = nt(AX[4, side], grads)
        g5 = nt(AX[5, 0], grads)
        OU[side, :, 896:1024] = jnp.where(lane < 64, g3, jnp.where(lane < 96, g4, g5)).astype(BF)

    def upper_gradient(level):
        await_grads(level)
        w, col = WIDTH[level], COLUMN[level]
        for side in range(2):
            OU[side, :, col : col + w] = nt(AX[level, side], GX[side, col : col + w, :]).astype(BF)

    upper_gradient(2)

    leaf_back((1, 2))
    partial_sums((3,))

    rows = at(p, 256)
    OU[c, :, 0:512] = nt(H0[rows, :], GX[c, 0:512, :]).astype(BF)
    OU[1 - c, :, 0:512] = nt(AX[0, 1 - c], GX[1 - c, 0:512, :]).astype(BF)

    leaf_back((3,))

    upper_gradient(1)

    await_bytes(XS.at[0:3], x1s)
    await_bytes(CS.at[0:3], x3s)
    await_bytes(H0.at[:, 0 : 3 * B], h0s)
    await_bytes(MS, pss)
    for level in range(1, LEVELS - 1):
        await_bytes(BO.at[level - 1], bos.at[level])
    await_bytes(CF.at[0:3, 0, 0], cfs.at[0])
    await_bytes(CF.at[0:3, :, 0], cfs.at[1])
    await_bytes(CF.at[:, :, 0], cfs.at[2])
    await_bytes(WF.at[0:3, 0, 0], w1s)
    await_bytes(WF.at[:, :, 0, 0], w2s)
    await_bytes(WF.at[0:2, :, 0, 0], w3s)
    await_bytes(WF.at[:, :, 0], w4s)
    for level in range(LEVELS + 1):
        if level < LEVELS:
            half = GROUP[level] // 2
            block = A[level].shape[0] // GROUP[level]
            await_bytes(A[level].at[0 : half * block], fs.at[level])
            if half > 1:
                await_bytes(A[level].at[0 : (half - 1) * block], ff.at[level])
        if 0 < level < LEVELS - 1:
            await_bytes(BS[level].at[0 : BS[level].shape[0] - 1], bs.at[level])
        if level:
            await_bytes(passed(level), axs.at[level])
            w, col = WIDTH[level], COLUMN[level]
            await_bytes(GX.at[:, col : col + w, 0 : 3 * B], gxs.at[level])
        await_bytes(passed(level), aps.at[level])
    await_bytes(GX.at[:, 0:512, 0 : 2 * B], gxs.at[0])
    await_bytes(GX.at[:, 0:512, own], gxt)


def scratch():
    vm = pltpu.VMEM
    dma = pltpu.SemaphoreType.DMA
    chunks = [vm((GROUP[j] // 2, CHUNK[j] + 16, B), BF) for j in range(1, LEVELS - 1)]
    return (
        [
            vm((2048, F), BF), vm((256, 256), BF), vm((4, 4, B, F), BF), vm((4, ALL, F), BF),
            vm((4, F, D), BF), vm((4, D, F), BF), vm((D, D), BF), vm((D, D), BF),
            vm((4, 128, 2, D), BF), vm((2, D, D), BF), vm((4, 4, 2, 32, B), F32),
            vm((4, D, ALL), BF), vm((8, ALL), F32),
            vm((4, D, B), BF), vm((4, D, B), BF),
        ]
        + [vm((2 * D, B), BF)] * 5
        + [vm((D, B), BF)]
        + [vm((D, B), F32)] * 3
        + [vm((1, 2, 128, B), BF), vm((2, 384, B), BF), vm((2, 2, D, 128), BF)]
        + [vm((3, 2, 528, B), BF)] * 2
        + chunks
        + chunks
        + [
            vm((2, D, ALL), BF), vm((6, 2, 256, ALL), BF), vm((4, D, B), BF),
            vm((D, 2 * B), F32),
            vm((D, ALL), BF), vm((D, ALL), BF), vm((8, ALL), F32),
            vm((4, D, B), BF), vm((D, 2 * B), F32),
            vm((4, 4, 2, 2, 64, D), BF), vm((128, D), BF), vm((2, D, B), F32), vm((2, D, B), BF), vm((D, B), F32),
        ]
        + [
            dma((8,)), dma((22,)), dma, dma((4,)), dma, dma, dma, dma, dma, dma,
            dma((6,)), dma((6, 16)), dma((6,)), dma((6,)), dma((6,)), dma((6,)), dma((6,)), dma((6,)),
            dma((6,)), dma((6,)), dma((6,)), dma((6,)), dma((6,)), dma((6,)), dma((4, 2)), dma, dma, dma((4,)),
            dma((3,)), dma((3,)), dma, dma((2,)), dma, dma((2, 2)), dma, dma((2, 2)), dma, dma,
        ]
    )


def gradients(CT, LM, CR, XT, OU, lg_hbm, mg_hbm, ug_hbm, LW, OM, OI, sem):
    copies = []

    def out(src, dst):
        copies.append(pltpu.make_async_copy(src, dst, sem.at[len(copies)]))
        copies[-1].start()

    for t in range(4):
        rows = slice(64 * t, 64 * (t + 1))
        for side in range(2):
            OI[rows, side, :] = OU[side, rows, :]
    out(OI, ug_hbm)
    for k in range(4):
        LW[k] = nt(XT[k], CT[k]).astype(BF)
        out(LW.at[k], lg_hbm.at[k])
    for t in range(4):
        rows = slice(256 * t, 256 * (t + 1))
        OM[rows, :] = nt(LM[rows, :], CR[...]).astype(BF)
        out(OM.at[rows], mg_hbm.at[rows])
    for copy in copies:
        copy.wait()


def on_device(regions, leaf_map, leaf_bond_weight, mid_weight, upper_weight, head_cotangent):
    anywhere = pl.BlockSpec(memory_space=pl.ANY)
    local = pl.BlockSpec(memory_space=pltpu.VMEM)
    kept = pl.pallas_call(
        kernel,
        out_shape=(
            pltpu.VMEM((4, D, ALL), BF),
            pltpu.VMEM((D, ALL), BF),
            pltpu.VMEM((D, ALL), BF),
            pltpu.VMEM((4, F, ALL), BF),
            pltpu.VMEM((2, 256, D), BF),
        ),
        in_specs=[pl.BlockSpec(memory_space=pltpu.SMEM)] + [anywhere] * 5,
        out_specs=(local,) * 5,
        scratch_shapes=scratch(),
        compiler_params=pltpu.CompilerParams(
            collective_id=0, has_side_effects=True, vmem_limit_bytes=VMEM_LIMIT
        ),
    )(
        leaf_map, regions.reshape(B * 16, F), leaf_bond_weight[0], mid_weight[0, 0],
        upper_weight[0], head_cotangent.T,
    )
    kept = [pltpu.with_memory_space_constraint(array, pltpu.VMEM) for array in kept]
    outs = pl.pallas_call(
        gradients,
        out_shape=(
            jax.ShapeDtypeStruct((4, F, D), BF),
            jax.ShapeDtypeStruct((D, D), BF),
            jax.ShapeDtypeStruct((256, 2, D), BF),
        ),
        in_specs=[local] * 5,
        out_specs=(anywhere,) * 3,
        scratch_shapes=[
            pltpu.VMEM((4, F, D), BF), pltpu.VMEM((D, D), BF), pltpu.VMEM((256, 2, D), BF),
            pltpu.SemaphoreType.DMA((9,)),
        ],
        compiler_params=pltpu.CompilerParams(vmem_limit_bytes=32000000),
    )(*kept)
    return (outs[0][None], outs[1][None, None], outs[2][None])


def solution(mesh):
    placed = (
        P("rep", "sub", None),
        P("sub"),
        P(("sub", "rep"), None, None, None),
        P("sub", "rep", None, None),
        P("sub", None, None, None),
        P("rep", "sub"),
    )
    return jax.shard_map(
        on_device,
        mesh=mesh,
        in_specs=placed,
        out_specs=(
            P(("sub", "rep"), None, None, None),
            P("sub", "rep", None, None),
            P("sub", "rep", None, None),
        ),
        check_vma=False,
    )
```

profile of v0, /device:TPU:1, one launch (start us, length us, event | category | flops | bytes accessed | tf_op | source)
XLA Modules:
  0.0 110.5 jit_solution(6478771715930983135)
XLA Ops:
  0.6 106.0 %shard_map.85 = (bf16[4,1024,512]{2,1,0:T(8,128)(2,1)S(1)}, bf16[1024,512]{1,0:T(8,128)(2,1)S(1)}, bf16[1024,512]{1,0:T(8,128)(2,1)S(1)}, bf16[4,256,512]{2,1,0:T(8,128)(2,1)S(1)}, bf16[2,256,1024]{2,1,0:T(8,128)(2,1)S(1)}) custom-call(s32[16]{0:T(128)} %map_ref.1, bf16[2048,256]{1,0:T(8,128)(2,1)} %bitcast.11, bf16[4,256,1024]{2,1,0:T(8,128)(2,1)} %bitcast.9, ...), custom_call_target="tpu_custom_call" | custom-call | tf_op jit(solution)/shard_map/pallas_call | solution.py:821
  106.7 3.6 %shard_map.86 = (bf16[4,256,1024]{2,1,0:T(8,128)(2,1)}, bf16[1024,1024]{1,0:T(8,128)(2,1)}, bf16[256,2,1024]{2,1,0:T(2,128)(2,1)}) custom-call(bf16[4,1024,512]{2,1,0:T(8,128)(2,1)S(1)} %get-tuple-element.11.CT, bf16[1024,512]{1,0:T(8,128)(2,1)S(1)} %get-tuple-element.12.LM, bf16[1024,512]{1,0:T(8,128)(2,1)S(1)} %get-tuple-element.13.CR, ...), custom_call_target="tpu_custom_call" | custom-call | tf_op jit(solution)/shard_map/pallas_call | solution.py:841
where the time goes:
time: 111 us; the launch traced here: 110 us
  Pallas kernels  110 us (99%)
    pallas_call x1, Pallas kernels, on_device(): pl.pallas_call(kernel, out_shape=(pltpu.VMEM((4, D, ALL), BF), pltpu.VMEM...  106 us
    pallas_call x1, Pallas kernels, on_device(): pl.pallas_call(gradients, out_shape=(jax.ShapeDtypeStruct((4, F, D), BF),...  3.62 us

commit v1 on v0

--- a/solution.py
+++ b/solution.py
@@ -130,20 +130,17 @@
 
     barrier = pltpu.get_barrier_semaphore()
 
-    def greet_sub(i, carry):
-        pl.semaphore_signal(
-            barrier, inc=1, device_id={"sub": lax.rem(s + i, SUBS)}, device_id_type=MESH
-        )
-        return carry
-
-    def greet_rep(i, carry):
+    def chip(dy, dz):
+        return (lax.rem(y + dy, 4) * 4 + lax.rem(z + dz, 4)) * 2 + c
+
+    far_first = list(reversed(steps_of(LEVELS - 1)))
+    for dy, dz in far_first:
+        pl.semaphore_signal(barrier, inc=1, device_id={"sub": chip(dy, dz)}, device_id_type=MESH)
+    for i in (2, 1, 3):
         pl.semaphore_signal(
             barrier, inc=1, device_id={"rep": lax.rem(p + i, REPS)}, device_id_type=MESH
         )
-        return carry
-
-    lax.fori_loop(1, SUBS, greet_sub, 0)
-    lax.fori_loop(1, REPS, greet_rep, 0)
+    pl.semaphore_signal(barrier, inc=1, device_id={"sub": partner}, device_id_type=MESH)
 
     column = lax.broadcasted_iota(jnp.int32, (16, 256), 1)
     sample = lax.broadcasted_iota(jnp.int32, (16, 256), 0)
@@ -156,7 +153,7 @@
         got = nn(Q[...], R[256 * q : 256 * (q + 1), :]).astype(BF)
         for l in range(16):
             XS[l // 4, l % 4, 16 * q : 16 * q + 16, :] = got[16 * l : 16 * l + 16, :]
-    pl.semaphore_wait(barrier, SUBS - 1 + REPS - 1)
+    pl.semaphore_wait(barrier, len(far_first) + 1 + REPS - 1)
 
     def source(i):
         return lax.rem(p + OFFSET[i], REPS)
@@ -178,9 +175,6 @@
         for t in range(4):
             rows = slice(256 * t, 256 * (t + 1))
             WF[y, z, c, side, :, rows] = WN[side, rows, 896:1024].T[64:128, :]
-
-    def chip(dy, dz):
-        return (lax.rem(y + dy, 4) * 4 + lax.rem(z + dz, 4)) * 2 + c
 
     for k in range(1, 4):
         ref = WF.at[y, z, c, 0]
@@ -595,6 +589,7 @@
         if level == 0:
             share_last_grads()
             break
+        share_grads(level)
         chunk = CHUNK[level]
         dots = [column_sum(dl), column_sum(dr)]
 
@@ -621,8 +616,6 @@
             BS[level][chunks, 0:chunk, :] = value.reshape(quarter, chunk, B)
             BS[level][chunks, chunk : chunk + 16, :] = jnp.broadcast_to(tile[None], (quarter, 16, B))
         own_chunk = scatter(level, lax.rem(s, group))
-        if level > 1:
-            share_grads(level)
         for done in {3: (0, 1, 2), 2: (3, 4), 1: (5,)}[level]:
             pass_rows(done)
 
@@ -650,9 +643,7 @@
     for i in range(REPS):
         R0[:, lanes_of(i)] = jnp.broadcast_to(factor_of(squares_of(H0, 0, lanes_of(i))), (8, B))
 
-    def leaf_back(blocks):
-        lanes = slice(blocks[0] * B, (blocks[-1] + 1) * B)
-        n = B * len(blocks)
+    def middle_back(blocks):
         for i in blocks:
             await_bytes(PR.at[i], prs.at[i])
         for b, i in enumerate(blocks):
@@ -669,6 +660,10 @@
                 rows = slice(128 * t, 128 * (t + 1))
                 v = PM[rows, part] - H0[rows, lanes_of(i)].astype(F32) * shift
                 CR[rows, lanes_of(i)] = (v * LO[rows, lanes_of(i)].astype(F32)).astype(BF)
+
+    def leaf_back(blocks):
+        lanes = slice(blocks[0] * B, (blocks[-1] + 1) * B)
+        n = B * len(blocks)
         total = jnp.zeros((8, n), F32)
         for t in range(4):
             rows = slice(256 * t, 256 * (t + 1))
@@ -688,10 +683,9 @@
         w, col = WIDTH[level], COLUMN[level]
         await_bytes(GX.at[:, col : col + w, 0 : 3 * B], gxr.at[level])
 
+    middle_back((0,))
     leaf_back((0,))
     relay_last_grads()
-    share_grads(1)
-    partial_sums((1, 2))
 
     for copy in kept:
         copy.wait()
@@ -714,17 +708,19 @@
             OU[side, :, col : col + w] = nt(AX[level, side], GX[side, col : col + w, :]).astype(BF)
 
     upper_gradient(2)
-
+    upper_gradient(1)
+
+    partial_sums((1, 2))
+    middle_back((1, 2))
+    partial_sums((3,))
     leaf_back((1, 2))
-    partial_sums((3,))
 
     rows = at(p, 256)
     OU[c, :, 0:512] = nt(H0[rows, :], GX[c, 0:512, :]).astype(BF)
     OU[1 - c, :, 0:512] = nt(AX[0, 1 - c], GX[1 - c, 0:512, :]).astype(BF)
 
+    middle_back((3,))
     leaf_back((3,))
-
-    upper_gradient(1)
 
     await_bytes(XS.at[0:3], x1s)
     await_bytes(CS.at[0:3], x3s)

time: 111 us -> 110 us (level)
  no operation moved by 1% of the time
where the time goes in v1:
time: 110 us
  Pallas kernels  109 us (99%)
    pallas_call x1, Pallas kernels, on_device(): pl.pallas_call(kernel, out_shape=(pltpu.VMEM((4, D, ALL), BF), pltpu.VMEM...  105 us
    pallas_call x1, Pallas kernels, on_device(): pl.pallas_call(gradients, out_shape=(jax.ShapeDtypeStruct((4, F, D), BF),...  3.62 us

profile of v1, /device:TPU:1, one launch (start us, length us, event | category | flops | bytes accessed | tf_op | source)
XLA Modules:
  0.0 109.6 jit_solution(16144327662961023972)
XLA Ops:
  0.6 105.1 %shard_map.85 = (bf16[4,1024,512]{2,1,0:T(8,128)(2,1)S(1)}, bf16[1024,512]{1,0:T(8,128)(2,1)S(1)}, bf16[1024,512]{1,0:T(8,128)(2,1)S(1)}, bf16[4,256,512]{2,1,0:T(8,128)(2,1)S(1)}, bf16[2,256,1024]{2,1,0:T(8,128)(2,1)S(1)}) custom-call(s32[16]{0:T(128)} %map_ref.1, bf16[2048,256]{1,0:T(8,128)(2,1)} %bitcast.11, bf16[4,256,1024]{2,1,0:T(8,128)(2,1)} %bitcast.9, ...), custom_call_target="tpu_custom_call" | custom-call | tf_op jit(solution)/shard_map/pallas_call | solution.py:817
  105.8 3.6 %shard_map.86 = (bf16[4,256,1024]{2,1,0:T(8,128)(2,1)}, bf16[1024,1024]{1,0:T(8,128)(2,1)}, bf16[256,2,1024]{2,1,0:T(2,128)(2,1)}) custom-call(bf16[4,1024,512]{2,1,0:T(8,128)(2,1)S(1)} %get-tuple-element.11.CT, bf16[1024,512]{1,0:T(8,128)(2,1)S(1)} %get-tuple-element.12.LM, bf16[1024,512]{1,0:T(8,128)(2,1)S(1)} %get-tuple-element.13.CR, ...), custom_call_target="tpu_custom_call" | custom-call | tf_op jit(solution)/shard_map/pallas_call | solution.py:837

commit v2 on v1

--- a/solution.py
+++ b/solution.py
@@ -604,7 +604,7 @@
         for side in range(2):
             BO[level - 1, side, 0:512, :] = half_sums(side, 1 - c).astype(BF)
             BO[level - 1, side, 512:528, :] = split_tile(dots[side])
-        to_sub(BO.at[level - 1], BI.at[level - 1], bos.at[level], bis.at[level], partner)
+            to_sub(BO.at[level - 1, side], BI.at[level - 1, side], bos.at[level], bis.at[level], partner)
         for side in range(2):
             LB[side * 512 : (side + 1) * 512, 0:B] = half_sums(side, c)
         await_bytes(BI.at[level - 1], bis.at[level])
@@ -795,14 +795,13 @@
         copies.append(pltpu.make_async_copy(src, dst, sem.at[len(copies)]))
         copies[-1].start()
 
-    for t in range(4):
-        rows = slice(64 * t, 64 * (t + 1))
+    for k in range(4):
+        rows = slice(64 * k, 64 * (k + 1))
         for side in range(2):
             OI[rows, side, :] = OU[side, rows, :]
-    out(OI, ug_hbm)
-    for k in range(4):
         LW[k] = nt(XT[k], CT[k]).astype(BF)
         out(LW.at[k], lg_hbm.at[k])
+    out(OI, ug_hbm)
     for t in range(4):
         rows = slice(256 * t, 256 * (t + 1))
         OM[rows, :] = nt(LM[rows, :], CR[...]).astype(BF)

time: 110 us -> 110 us (level)
  no operation moved by 1% of the time
where the time goes in v2:
time: 110 us
  Pallas kernels  109 us (99%)
    pallas_call x1, Pallas kernels, on_device(): pl.pallas_call(kernel, out_shape=(pltpu.VMEM((4, D, ALL), BF), pltpu.VMEM...  105 us
    pallas_call x1, Pallas kernels, on_device(): pl.pallas_call(gradients, out_shape=(jax.ShapeDtypeStruct((4, F, D), BF),...  3.74 us

profile of v2, /device:TPU:1, one launch (start us, length us, event | category | flops | bytes accessed | tf_op | source)
XLA Modules:
  0.0 109.8 jit_solution(9826418403706725168)
XLA Ops:
  0.6 105.2 %shard_map.85 = (bf16[4,1024,512]{2,1,0:T(8,128)(2,1)S(1)}, bf16[1024,512]{1,0:T(8,128)(2,1)S(1)}, bf16[1024,512]{1,0:T(8,128)(2,1)S(1)}, bf16[4,256,512]{2,1,0:T(8,128)(2,1)S(1)}, bf16[2,256,1024]{2,1,0:T(8,128)(2,1)S(1)}) custom-call(s32[16]{0:T(128)} %map_ref.1, bf16[2048,256]{1,0:T(8,128)(2,1)} %bitcast.11, bf16[4,256,1024]{2,1,0:T(8,128)(2,1)} %bitcast.9, ...), custom_call_target="tpu_custom_call" | custom-call | tf_op jit(solution)/shard_map/pallas_call | solution.py:816
  105.8 3.7 %shard_map.86 = (bf16[4,256,1024]{2,1,0:T(8,128)(2,1)}, bf16[1024,1024]{1,0:T(8,128)(2,1)}, bf16[256,2,1024]{2,1,0:T(2,128)(2,1)}) custom-call(bf16[4,1024,512]{2,1,0:T(8,128)(2,1)S(1)} %get-tuple-element.11.CT, bf16[1024,512]{1,0:T(8,128)(2,1)S(1)} %get-tuple-element.12.LM, bf16[1024,512]{1,0:T(8,128)(2,1)S(1)} %get-tuple-element.13.CR, ...), custom_call_target="tpu_custom_call" | custom-call | tf_op jit(solution)/shard_map/pallas_call | solution.py:836
